TPU v7x, 512 devices: a whole 4x4x16 slice. The times are simulated.
512 devices in a mesh: row: 16 (over y, x), col: 32 (over z, core).
Axes of the slice: x: 4, y: 4, z: 16, core: 2. Of those that a mesh axis runs over, the one named last changes fastest.
Arguments:
- root_inverse: bfloat16 [4096, 4096], P('row', 'col'), may hold values from -16 to 16
- factor: bfloat16 [4096, 4, 4096], P('row', None, 'col'), may hold values from -0.59765625 to 0.59765625
- inverse_diag: bfloat16 [4096, 4, 4096], P('row', None, 'col'), may hold values from -6 to 6
- structure: int32 [4, 32], replicated, may hold values 0 or 1
Outputs:
- ainv_rk: bfloat16 [4096, 4, 4096], P('row', None, 'col')
- ainv_kk: bfloat16 [4096, 4, 4096], P('row', None, 'col')
All inputs are finite; a program needn't handle non-finite values.
Results may differ from a plain program's by a relative error of at most 0.014.
Values may be sent and summed in bfloat16 or wider, within the bound.
No kernel may reach another device: no remote copies, remote signals or barrier semaphores. Data moves between devices by JAX's collectives and lax.ppermute only.
A program may use at most 64 MiB of HBM per device.

v0:
```python
import jax
import jax.numpy as jnp
from jax import lax
from jax.sharding import PartitionSpec as P

BLK = 128


def body(root_inverse, factor, inverse_diag, structure):
    local_rows = factor.shape[0]
    offset = lax.axis_index("row") * local_rows
    row_mask = jnp.repeat(structure, BLK, axis=1)
    local_mask = lax.dynamic_slice_in_dim(row_mask, offset, local_rows, 1).T.astype(factor.dtype)
    masked = factor * local_mask[:, :, None]
    root_rows = lax.all_gather(root_inverse, "col", axis=1, tiled=True)
    product = jnp.einsum(
        "ik,knj->inj",
        root_rows,
        lax.all_gather(masked, "row", axis=0, tiled=True),
        preferred_element_type=jnp.float32,
    )
    ainv_rk = (-product).astype(jnp.bfloat16)
    inverse_rows = lax.all_gather(ainv_rk, "col", axis=2, tiled=True)
    running = lax.psum_scatter(
        jnp.einsum("kni,knj->inj", inverse_rows, masked, preferred_element_type=jnp.float32).astype(
            jnp.bfloat16
        ),
        "row",
        scatter_dimension=0,
        tiled=True,
    ).astype(jnp.float32)
    ainv_kk = (inverse_diag.astype(jnp.float32) - running).astype(jnp.bfloat16)
    return (ainv_rk, ainv_kk)


def solution(mesh):
    return jax.shard_map(
        body,
        mesh=mesh,
        in_specs=(P("row", "col"), P("row", None, "col"), P("row", None, "col"), P()),
        out_specs=(P("row", None, "col"), P("row", None, "col")),
        check_vma=False,
    )
```

profile of v0, /device:TPU:32, one launch (start us, length us, event | category | flops | bytes accessed | tf_op | source)
XLA Modules:
  0.0 349.0 jit_solution(17044077061663513549)
XLA Ops:
  7.2 0.0 copy-start
  7.2 0.0 all-gather.6.cloned.1.call-start
  7.2 0.7 all-gather.6.cloned.1.call-update
  7.9 0.0 all-gather.4.cloned.1.call-start
  8.0 0.0 copy-done
  8.0 0.1 broadcast_bitcast_fusion
  8.0 0.1 copy.14
  8.1 1.1 copy.6
  9.2 0.7 broadcast_multiply_fusion
  10.0 0.0 all-gather.4.cloned.1.call-update
  10.0 0.0 copy-start.1
  10.0 0.0 all-gather.8.cloned.1.call-start
  10.0 76.9 %all-gather.6.cloned.1.call-done = bf16[256,4096]{1,0:T(8,128)(2,1)} async-done(((bf16[256,128]{1,0:T(8,128)(2,1)}), bf16[256,4096]{1,0:T(8,128)(2,1)}) %all-gather.6.cloned.1.call-update) | async-done | bytes 2097168 | tf_op jit(solution)/shard_map/all_gather | solution.py:15
  86.9 71.7 %all-gather.4.cloned.1.call-done = bf16[4096,4,128]{0,2,1:T(8,128)(2,1)} async-done(((bf16[256,4,128]{0,2,1:T(8,128)(2,1)}), bf16[4096,4,128]{0,2,1:T(8,128)(2,1)}) %all-gather.4.cloned.1.call-update) | async-done | bytes 4194320 | tf_op jit(solution)/shard_map/all_gather | solution.py:19
  158.6 4.9 %fusion.9 = bf16[256,4,128]{0,2,1:T(8,128)(2,1)} fusion(bf16[4096,4,128]{0,2,1:T(8,128)(2,1)} %all-gather.4.cloned.1.call-done, bf16[256,4096]{1,0:T(8,128)(2,1)} %all-gather.6.cloned.1.call-done), kind=kOutput, calls=%fused_computation.6 | convolution fusion | flops 1074003968 | bytes 6553600 | tf_op jit(solution)/shard_map/ik,knj->inj/dot_general | solution.py:16
  163.5 0.0 all-gather.8.cloned.1.call-update
  163.5 0.0 reduce-scatter.2.cloned.1.call-start
  163.5 78.3 %all-gather.8.cloned.1.call-done = bf16[256,4,4096]{0,2,1:T(8,128)(2,1)} async-done(((bf16[256,4,128]{0,2,1:T(8,128)(2,1)}), bf16[256,4,4096]{0,2,1:T(8,128)(2,1)}) %all-gather.8.cloned.1.call-update) | async-done | bytes 8388624 | tf_op jit(solution)/shard_map/all_gather | solution.py:23
  241.9 0.0 copy-done.1
  241.9 8.2 %fusion = bf16[4096,4,128]{0,2,1:T(8,128)(2,1)} fusion(bf16[256,4,128]{0,2,1:T(8,128)(2,1)S(1)} %copy-done.1, bf16[256,4,4096]{0,2,1:T(8,128)(2,1)} %all-gather.8.cloned.1.call-done), kind=kOutput, calls=%fused_computation.1 | convolution fusion | flops 1075838976 | bytes 12845056 | tf_op jit(solution)/shard_map/kni,knj->inj/dot_general | solution.py:25
  250.1 0.0 copy-start.3
  250.1 0.0 copy-start.2
  250.1 0.0 reduce-scatter.2.cloned.1.call-update
  250.1 0.9 copy-done.3
  251.0 0.2 copy.7
  251.2 0.0 copy-done.2
  251.2 0.9 copy.9
  252.1 88.5 %reduce-scatter.2.cloned.1.call-done = bf16[256,4,128]{0,2,1:T(8,128)(2,1)} async-done(((bf16[4096,4,128]{0,2,1:T(8,128)(2,1)}), bf16[256,4,128]{0,2,1:T(8,128)(2,1)}) %reduce-scatter.2.cloned.1.call-update) | async-done | bytes 262160 | tf_op jit(solution)/shard_map/reduce_scatter | solution.py:24
  340.6 1.0 subtract_convert_fusion
  341.6 0.9 copy.10
  (1 shorter events, 0.0 us)
Async XLA Ops:
  7.2 0.8 copy-start
  7.2 79.7 %all-gather.6.cloned.1.call-start = ((), (), s32[]{:S(2)}) async-start(), calls=%async_computation.2 | async-start | bytes 2162688 | tf_op jit(solution)/shard_map/all_gather | solution.py:15
  7.9 150.7 %all-gather.4.cloned.1.call-start = ((), (), s32[]{:S(2)}) async-start(), calls=%async_computation.1 | async-start | bytes 4456448 | tf_op jit(solution)/shard_map/all_gather | solution.py:19
  10.0 231.9 %copy-start.1 = (bf16[256,4,128]{0,2,1:T(8,128)(2,1)S(1)}, bf16[256,4,128]{0,2,1:T(8,128)(2,1)}, u32[]{:S(2)}) copy-start(bf16[256,4,128]{0,2,1:T(8,128)(2,1)} %broadcast_multiply_fusion) | copy-start | bytes 786436
  10.0 231.9 %all-gather.8.cloned.1.call-start = ((), (), s32[]{:S(2)}) async-start(), calls=%async_computation.3 | async-start | bytes 8650752 | tf_op jit(solution)/shard_map/all_gather | solution.py:23
  163.5 177.1 %reduce-scatter.2.cloned.1.call-start = ((), (), s32[]{:S(2)}) async-start(), calls=%async_computation.4 | async-start | bytes 4456448 | tf_op jit(solution)/shard_map/reduce_scatter | solution.py:24
  250.1 0.9 copy-start.3
  250.1 1.1 copy-start.2
Sparse Core Ops, SparseCore 0:
  10.0 76.8 all-gather.5
  90.5 68.0 all-gather.3
  163.6 78.2 all-gather.7
  250.2 90.3 reduce-scatter.1
where the time goes:
time: 349 us
  waiting for transfers between devices  316 us (91%)
  between operations  13.8 us (4%)
  matrix products  13 us (4%)
  local copies, waits for them, and re-layouts  4.08 us (1%)
    reduce_scatter x1, waiting for transfers between devices, body(): lax.psum_scatter(jnp.einsum('kni,knj->inj', inverse_rows, masked, preferr...  88.5 us
    all_gather x1, waiting for transfers between devices, body(): inverse_rows = lax.all_gather(ainv_rk, 'col', axis=2, tiled=True)  78.3 us
    all_gather x1, waiting for transfers between devices, body(): root_rows = lax.all_gather(root_inverse, 'col', axis=1, tiled=True)  76.9 us
    all_gather x1, waiting for transfers between devices, body(): lax.all_gather(masked, 'row', axis=0, tiled=True)  71.7 us
    dot_general x1, matrix products, body(): jnp.einsum('kni,knj->inj', inverse_rows, masked, preferred_element_type=j...  8.19 us
  transfers between devices with their start and end apart: 4, of which 4 were waited for; matrix products, arithmetic and copies ran while one was open for 1% of the time, Pallas kernels for 0%

commit v1 on v0

v1 whole, which is shorter than its diff:
```python
import jax
import jax.numpy as jnp
from jax import lax
from jax.experimental import pallas as pl
from jax.experimental.pallas import tpu as pltpu
from jax.sharding import PartitionSpec as P

BLK = 128
CHUNKS = 8
VMEM_FIRST, VMEM_ROOT, VMEM_KID = 63, 57, 57
ANY = pl.BlockSpec(memory_space=pl.ANY)
VMEM = pl.BlockSpec(memory_space=pltpu.VMEM)
SMEM = pl.BlockSpec(memory_space=pltpu.SMEM)


def split_kids(flat_ref, kids_ref, flat_buf, wide_ref, sem):
    kids, rows, _ = kids_ref.shape
    copy = pltpu.make_async_copy(flat_ref, flat_buf, sem)
    copy.start()
    copy.wait()
    wide_ref[...] = flat_buf[...].astype(jnp.float32)
    for n in range(kids):
        kids_ref[n] = wide_ref[pl.ds(n, rows, stride=kids), :].astype(kids_ref.dtype)


def root_product(
    keep_ref, row_ref, panel_ref, ainv_ref, turned_ref, row_buf, root_buf, acc_ref, wide_ref, sems
):
    n_row, kids, depth, cols = row_buf.shape
    last = panel_ref.shape[1] - 1
    g, c = n_row // CHUNKS, root_buf.shape[0] // CHUNKS

    def row_copy(s):
        return pltpu.make_async_copy(
            row_ref.at[pl.ds(s * g, g)], row_buf.at[pl.ds(s * g, g)], sems.at[0, s]
        )

    def root_copy(s):
        return pltpu.make_async_copy(
            panel_ref.at[pl.ds(s * c, c), last], root_buf.at[pl.ds(s * c, c)], sems.at[1, s]
        )

    for s in range(CHUNKS):
        row_copy(s).start()
        root_copy(s).start()
    acc_ref[...] = jnp.zeros_like(acc_ref)

    @pl.loop(0, CHUNKS)
    def _(s):
        row_copy(s).wait()
        root_copy(s).wait()
        left = jnp.concatenate([root_buf[s * c + i] for i in range(c)], axis=1)
        right = jnp.concatenate(
            [
                jnp.concatenate([row_buf[s * g + i, n] for n in range(kids)], axis=1)
                for i in range(g)
            ],
            axis=0,
        )
        acc_ref[...] += jnp.dot(left, right, preferred_element_type=jnp.float32)

    for n in range(kids):
        value = (-acc_ref[:, n * cols : (n + 1) * cols]).astype(turned_ref.dtype)
        wide_ref[pl.ds(n, depth, stride=kids), :] = value.astype(jnp.float32)
        for b in range(depth // BLK):
            kept = jnp.where(keep_ref[n, b] != 0, value[b * BLK : (b + 1) * BLK], 0)
            turned_ref[n, :, b * BLK : (b + 1) * BLK] = kept.astype(turned_ref.dtype).T
    ainv_ref[...] = wide_ref[...].astype(ainv_ref.dtype)


def kid_product(turned_ref, panel_ref, part_ref, panel_buf, sems):
    n_col, groups, _, _ = panel_buf.shape
    c = n_col // CHUNKS

    def panel_copy(s):
        return pltpu.make_async_copy(
            panel_ref.at[pl.ds(s * c, c), pl.ds(0, groups)],
            panel_buf.at[pl.ds(s * c, c)],
            sems.at[s],
        )

    for s in range(CHUNKS):
        panel_copy(s).start()
    left = jnp.concatenate([turned_ref[y] for y in range(groups)], axis=1)

    @pl.loop(0, CHUNKS)
    def _(s):
        panel_copy(s).wait()
        for i in range(c // 2):
            at = s * c + 2 * i
            right = jnp.concatenate(
                [
                    jnp.concatenate([panel_buf[at + h, y] for y in range(groups)], axis=0)
                    for h in range(2)
                ],
                axis=1,
            )
            part_ref[s * (c // 2) + i] = jnp.dot(
                left, right, preferred_element_type=jnp.float32
            ).astype(part_ref.dtype)


def finish(pieces_ref, diag_ref, kk_ref, wide_ref):
    n_row, _, depth = pieces_ref.shape
    kids = wide_ref.shape[0] // depth
    per = n_row // kids
    wide_ref[...] = diag_ref[...].astype(jnp.float32)
    for n in range(kids):
        total = pieces_ref[n * per].astype(jnp.float32)
        for r in range(1, per):
            total += pieces_ref[n * per + r].astype(jnp.float32)
        at = pl.ds(n, depth, stride=kids)
        wide_ref[at, :] = wide_ref[at, :] - total.T
    kk_ref[...] = wide_ref[...].astype(kk_ref.dtype)


def body(root_inverse, factor, inverse_diag, structure):
    rows, kids, cols = factor.shape
    dtype = factor.dtype
    n_row, n_col = lax.axis_size("row"), lax.axis_size("col")
    per, side = rows // BLK, n_row // kids
    flat = (rows * kids, cols)
    along = [[y * side + x for y in range(kids)] for x in range(side)]
    mine = pl.pallas_call(
        split_kids,
        out_shape=jax.ShapeDtypeStruct((kids, rows, cols), dtype),
        in_specs=[ANY],
        out_specs=VMEM,
        scratch_shapes=[
            pltpu.VMEM(flat, dtype),
            pltpu.VMEM(flat, jnp.float32),
            pltpu.SemaphoreType.DMA(()),
        ],
        compiler_params=pltpu.CompilerParams(vmem_limit_bytes=VMEM_FIRST << 20),
    )(factor.reshape(flat))
    kid = lax.all_to_all(mine, "row", 0, 0, axis_index_groups=along)
    panel = lax.all_gather(jnp.concatenate([kid, root_inverse[None]], axis=0), "col", axis=0)
    keep = lax.dynamic_slice_in_dim(structure, lax.axis_index("row") * per, per, 1)
    mask = jnp.repeat(keep, BLK, axis=1).astype(dtype)
    masked = mine * mask[:, :, None]
    row_m = lax.all_to_all(jnp.broadcast_to(masked[None], (n_row, kids, rows, cols)), "row", 0, 0)
    ainv, turned = pl.pallas_call(
        root_product,
        out_shape=(
            jax.ShapeDtypeStruct(flat, dtype),
            jax.ShapeDtypeStruct((kids, cols, rows), dtype),
        ),
        in_specs=[SMEM, ANY, ANY],
        out_specs=(VMEM, VMEM),
        scratch_shapes=[
            pltpu.VMEM((n_row, kids, rows, cols), dtype),
            pltpu.VMEM((n_col, rows, cols), dtype),
            pltpu.VMEM((rows, kids * cols), jnp.float32),
            pltpu.VMEM(flat, jnp.float32),
            pltpu.SemaphoreType.DMA((2, CHUNKS)),
        ],
        compiler_params=pltpu.CompilerParams(vmem_limit_bytes=VMEM_ROOT << 20),
        cost_estimate=pl.CostEstimate(
            flops=2 * n_row * rows * rows * kids * cols,
            bytes_accessed=6 << 20,
            transcendentals=0,
        ),
    )(keep, row_m, panel)
    turned = lax.all_to_all(turned, "row", 0, 0, axis_index_groups=along)
    part = pl.pallas_call(
        kid_product,
        out_shape=jax.ShapeDtypeStruct((n_row, cols, rows), dtype),
        in_specs=[VMEM, ANY],
        out_specs=VMEM,
        scratch_shapes=[
            pltpu.VMEM((n_col, kids, rows, cols), dtype),
            pltpu.SemaphoreType.DMA((CHUNKS,)),
        ],
        compiler_params=pltpu.CompilerParams(vmem_limit_bytes=VMEM_KID << 20),
        cost_estimate=pl.CostEstimate(
            flops=2 * n_row * rows * rows * kids * cols,
            bytes_accessed=9 << 20,
            transcendentals=0,
        ),
    )(turned, panel)
    pieces = lax.all_to_all(part, "row", 0, 0)
    ainv_kk = pl.pallas_call(
        finish,
        out_shape=jax.ShapeDtypeStruct(flat, dtype),
        in_specs=[VMEM, VMEM],
        out_specs=VMEM,
        scratch_shapes=[pltpu.VMEM(flat, jnp.float32)],
        compiler_params=pltpu.CompilerParams(vmem_limit_bytes=6 << 20),
    )(pieces, inverse_diag.reshape(flat))
    return (ainv.reshape(factor.shape), ainv_kk.reshape(factor.shape))


def solution(mesh):
    return jax.shard_map(
        body,
        mesh=mesh,
        in_specs=(P("row", "col"), P("row", None, "col"), P("row", None, "col"), P()),
        out_specs=(P("row", None, "col"), P("row", None, "col")),
        check_vma=False,
    )
```

time: 349 us -> 157 us (0.45)
  the two profiles are of different devices: /device:TPU:32 before, /device:TPU:2 now
where the time goes in v1:
time: 157 us
  blocking collectives  98.6 us (63%)
  waiting for transfers between devices  25.2 us (16%)
  between operations  14.1 us (9%)
  Pallas kernels  13.7 us (9%)
  other arithmetic  4.05 us (3%)
    all_to_all x1, blocking collectives, body(): lax.all_to_all(jnp.broadcast_to(masked[None], (n_row, kids, rows, cols)),...  55.3 us
    all_gather x1, waiting for transfers between devices, body(): lax.all_gather(jnp.concatenate([kid, root_inverse[None]], axis=0), 'col',...  25.1 us
    all_to_all x1, blocking collectives, body(): pieces = lax.all_to_all(part, 'row', 0, 0)  20.5 us
    all_to_all x1, blocking collectives, body(): turned = lax.all_to_all(turned, 'row', 0, 0, axis_index_groups=along)  11.6 us
    all_to_all x1, blocking collectives, body(): kid = lax.all_to_all(mine, 'row', 0, 0, axis_index_groups=along)  11.2 us
    pallas_call x1, Pallas kernels, body(): pl.pallas_call(kid_product, out_shape=jax.ShapeDtypeStruct((n_row, cols,...  5.79 us
    pallas_call x1, Pallas kernels, body(): pl.pallas_call(root_product, out_shape=(jax.ShapeDtypeStruct(flat, dtype)...  5.28 us
  transfers between devices with their start and end apart: 1, of which 1 were waited for; matrix products, arithmetic and copies ran while one was open for 2% of the time, Pallas kernels for 0%

profile of v1, /device:TPU:2, one launch (start us, length us, event | category | flops | bytes accessed | tf_op | source)
XLA Modules:
  0.0 156.8 jit_solution(16240533314812197282)
XLA Ops:
  7.2 0.0 all-gather.3.cloned.1.call-start
  7.2 1.7 %shard_map.59 = bf16[4,256,128]{2,1,0:T(8,128)(2,1)} custom-call(bf16[1024,128]{1,0:T(8,128)(2,1)} %bitcast.14), custom_call_target="tpu_custom_call" | custom-call | tf_op jit(solution)/shard_map/pallas_call | solution.py:124
  8.9 11.2 %all_to_all.20 = bf16[4,256,128]{2,1,0:T(8,128)(2,1)S(1)} all-to-all(bf16[4,256,128]{2,1,0:T(8,128)(2,1)} %shard_map.59), channel_id=1, replica_groups={{0,128,256,384},{32,160,288,416},{64,192,320,448},{96,224,352,480},{1,1..., dimensions={0} | all-to-all | bytes 524288 | tf_op jit(solution)/shard_map/all_to_all | solution.py:136
  20.1 1.6 %pad_maximum_fusion = bf16[5,256,128]{2,1,0:T(8,128)(2,1)} fusion(bf16[1,256,128]{2,1,0:T(8,128)(2,1)} %bitcast.16, bf16[4,256,128]{2,1,0:T(8,128)(2,1)S(1)} %all_to_all.20), kind=kLoop, calls=%fused_computation | loop fusion | flops 163840 | bytes 655360 | tf_op jit(solution)/shard_map/concatenate | solution.py:137
  21.7 0.0 all-gather.3.cloned.1.call-update
  21.7 1.3 fusion
  23.0 0.1 broadcast_bitcast_fusion
  23.1 1.1 broadcast_multiply_fusion
  24.3 1.0 broadcast_in_dim.14
  25.3 55.3 %all_to_all.21.row_ref = bf16[16,4,256,128]{3,2,1,0:T(8,128)(2,1)} all-to-all(bf16[16,4,256,128]{3,2,1,0:T(8,128)(2,1)S(1)} %broadcast_in_dim.14), channel_id=1, replica_groups=mesh['row'=16,'col'=32] {'row'}, dimensions={0} | all-to-all | bytes 8388608 | tf_op jit(solution)/shard_map/all_to_all | solution.py:141
  80.6 25.1 %all-gather.3.cloned.1.call-done = bf16[160,256,128]{2,1,0:T(8,128)(2,1)} async-done(((bf16[5,256,128]{2,1,0:T(8,128)(2,1)}), bf16[160,256,128]{2,1,0:T(8,128)(2,1)}) %all-gather.3.cloned.1.call-update) | async-done | bytes 10485776 | tf_op jit(solution)/shard_map/all_gather | solution.py:137
  105.8 5.3 %shard_map.60 = (bf16[1024,128]{1,0:T(8,128)(2,1)}, bf16[4,128,256]{2,1,0:T(8,128)(2,1)}) custom-call(s32[4,2]{1,0:T(4,128)} %get-tuple-element.7.keep_ref, bf16[16,4,256,128]{3,2,1,0:T(8,128)(2,1)} %all_to_all.21.row_ref, bf16[32,5,256,128]{3,2,1,0:T(8,128)(2,1)} %bitcast.12), custom_call_target="tpu_custom_call" | custom-call | flops 1073741824 | bytes 6291456 | tf_op jit(solution)/shard_map/pallas_call | solution.py:142
  111.0 11.6 %all_to_all.22.turned_ref = bf16[4,128,256]{2,1,0:T(8,128)(2,1)} all-to-all(bf16[4,128,256]{2,1,0:T(8,128)(2,1)} %get-tuple-element.5), channel_id=1, replica_groups={{0,128,256,384},{32,160,288,416},{64,192,320,448},{96,224,352,480},{1,1..., dimensions={0} | all-to-all | bytes 524288 | tf_op jit(solution)/shard_map/all_to_all | solution.py:164
  122.7 0.0 copy-start
  122.7 5.8 %shard_map.61 = bf16[16,128,256]{2,1,0:T(8,128)(2,1)} custom-call(bf16[4,128,256]{2,1,0:T(8,128)(2,1)} %all_to_all.22.turned_ref, bf16[32,5,256,128]{3,2,1,0:T(8,128)(2,1)} %bitcast.13), custom_call_target="tpu_custom_call" | custom-call | flops 1073741824 | bytes 9437184 | tf_op jit(solution)/shard_map/pallas_call | solution.py:165
  128.5 20.5 %all_to_all.23.pieces_ref = bf16[16,128,256]{2,1,0:T(8,128)(2,1)S(1)} all-to-all(bf16[16,128,256]{2,1,0:T(8,128)(2,1)} %shard_map.61), channel_id=1, replica_groups=mesh['row'=16,'col'=32] {'row'}, dimensions={0} | all-to-all | bytes 2097152 | tf_op jit(solution)/shard_map/all_to_all | solution.py:181
  148.9 0.0 copy-done
  149.0 1.0 shard_map.62
  (1 shorter events, 0.0 us)
Async XLA Ops:
  7.2 98.6 %all-gather.3.cloned.1.call-start = ((), (), s32[]{:S(2)}) async-start(), calls=%async_computation.4 | async-start | bytes 10813440 | tf_op jit(solution)/shard_map/all_gather | solution.py:137
  122.7 26.3 %copy-start = (bf16[256,4,128]{2,1,0:T(4,128)(2,1)S(1)}, bf16[256,4,128]{2,1,0:T(4,128)(2,1)}, u32[]{:S(2)}) copy-start(bf16[256,4,128]{2,1,0:T(4,128)(2,1)} %param.6) | copy-start | bytes 786436
Sparse Core Ops, SparseCore 0:
  21.8 83.8 all-gather.2

commit v2 on v1

v2 whole, which is shorter than its diff:
```python
import jax
import jax.numpy as jnp
from jax import lax
from jax.experimental import pallas as pl
from jax.experimental.pallas import tpu as pltpu
from jax.sharding import PartitionSpec as P

BLK = 128
CHUNKS = 8
HALVES = 2
VMEM_FIRST, VMEM_ROOT, VMEM_KID = 63, 50, 16
ANY = pl.BlockSpec(memory_space=pl.ANY)
VMEM = pl.BlockSpec(memory_space=pltpu.VMEM)
SMEM = pl.BlockSpec(memory_space=pltpu.SMEM)


def split_kids(flat_ref, root_ref, turned_ref, folded_ref, flat_buf, root_buf, wide_ref, sems):
    groups, half, rows = turned_ref.shape
    kids = groups // HALVES
    cols = root_buf.shape[1]
    flat_copy = pltpu.make_async_copy(flat_ref, flat_buf, sems.at[0])
    root_copy = pltpu.make_async_copy(root_ref, root_buf, sems.at[1])
    flat_copy.start()
    root_copy.start()
    flat_copy.wait()
    wide_ref[...] = flat_buf[...].astype(jnp.float32)
    for n in range(kids):
        across = wide_ref[pl.ds(n, rows, stride=kids), :].astype(turned_ref.dtype).T
        for h in range(HALVES):
            turned_ref[n * HALVES + h] = across[h * half : (h + 1) * half]
    root_copy.wait()
    folded_ref[:, :cols] = root_buf[: rows // 2]
    folded_ref[:, cols:] = root_buf[rows // 2 :]


def root_product(
    keep_ref, row_ref, panel_ref, ainv_ref, slots_ref, row_buf, root_buf, acc_ref, wide_ref, sems
):
    n_row, kids, depth, cols = row_buf.shape
    first = panel_ref.shape[1] - root_buf.shape[1]
    g, c = n_row // CHUNKS, root_buf.shape[0] // CHUNKS

    def row_copy(s):
        return pltpu.make_async_copy(
            row_ref.at[pl.ds(s * g, g)], row_buf.at[pl.ds(s * g, g)], sems.at[0, s]
        )

    def root_copy(s):
        return pltpu.make_async_copy(
            panel_ref.at[pl.ds(s * c, c), pl.ds(first, root_buf.shape[1])],
            root_buf.at[pl.ds(s * c, c)],
            sems.at[1, s],
        )

    for s in range(CHUNKS):
        row_copy(s).start()
        root_copy(s).start()
    acc_ref[...] = jnp.zeros_like(acc_ref)

    @pl.loop(0, CHUNKS)
    def _(s):
        row_copy(s).wait()
        root_copy(s).wait()
        left = jnp.concatenate(
            [
                jnp.concatenate(
                    [root_buf[s * c + i, :, h * cols : (h + 1) * cols] for i in range(c)], axis=1
                )
                for h in range(2)
            ],
            axis=0,
        )
        right = jnp.concatenate(
            [
                jnp.concatenate([row_buf[s * g + i, n] for n in range(kids)], axis=1)
                for i in range(g)
            ],
            axis=0,
        )
        acc_ref[...] += jnp.dot(left, right, preferred_element_type=jnp.float32)

    for n in range(kids):
        value = (-acc_ref[:, n * cols : (n + 1) * cols]).astype(slots_ref.dtype)
        wide_ref[pl.ds(n, depth, stride=kids), :] = value.astype(jnp.float32)
        for b in range(depth // BLK):
            at = slice(b * BLK, (b + 1) * BLK)
            kept = jnp.where(keep_ref[n, b] != 0, value[at], 0).astype(slots_ref.dtype)
            for h in range(HALVES):
                slots_ref[n * HALVES + h, at] = kept
    ainv_ref[...] = wide_ref[...].astype(ainv_ref.dtype)


def kid_product(slots_ref, panel_ref, part_ref):
    groups, depth, cols = slots_ref.shape
    n_row, tall, _ = part_ref.shape
    half = cols // HALVES
    c = panel_ref.shape[0] // CHUNKS
    right = slots_ref[...].reshape(groups * depth, cols)

    @pl.loop(0, CHUNKS)
    def _(s):
        left = jnp.concatenate(
            [
                jnp.concatenate(
                    [panel_ref[s * c + i, u * half : (u + 1) * half] for u in range(groups)],
                    axis=1,
                )
                for i in range(c)
            ],
            axis=0,
        )
        made = jnp.dot(left, right, preferred_element_type=jnp.float32).astype(part_ref.dtype)
        for i in range(c // 2):
            part_ref[s * (c // 2) + i] = made[i * tall : (i + 1) * tall]


def finish(pieces_ref, diag_ref, kk_ref, wide_ref):
    n_row, tall, cols = pieces_ref.shape
    depth = tall * HALVES
    kids = wide_ref.shape[0] // depth
    per = n_row // kids
    half = cols // HALVES
    wide_ref[...] = diag_ref[...].astype(jnp.float32)
    for n in range(kids):
        for h in range(HALVES):
            total = pieces_ref[n * per + h].astype(jnp.float32)
            for x in range(h + HALVES, per, HALVES):
                total += pieces_ref[n * per + x].astype(jnp.float32)
            for core in range(tall // half):
                at = pl.ds((core * cols + h * half) * kids + n, half, stride=kids)
                wide_ref[at, :] = wide_ref[at, :] - total[core * half : (core + 1) * half]
    kk_ref[...] = wide_ref[...].astype(kk_ref.dtype)


def body(root_inverse, factor, inverse_diag, structure):
    rows, kids, cols = factor.shape
    dtype = factor.dtype
    n_row, n_col = lax.axis_size("row"), lax.axis_size("col")
    per, side = rows // BLK, n_row // kids
    half, groups = cols // HALVES, kids * HALVES
    flat = (rows * kids, cols)
    along = [
        [y * side + x * HALVES + h for y in range(kids) for h in range(HALVES)]
        for x in range(side // HALVES)
    ]
    turned, folded = pl.pallas_call(
        split_kids,
        out_shape=(
            jax.ShapeDtypeStruct((groups, half, rows), dtype),
            jax.ShapeDtypeStruct((rows // 2, 2 * cols), dtype),
        ),
        in_specs=[ANY, ANY],
        out_specs=(VMEM, VMEM),
        scratch_shapes=[
            pltpu.VMEM(flat, dtype),
            pltpu.VMEM((rows, cols), dtype),
            pltpu.VMEM(flat, jnp.float32),
            pltpu.SemaphoreType.DMA((2,)),
        ],
        compiler_params=pltpu.CompilerParams(vmem_limit_bytes=VMEM_FIRST << 20),
    )(factor.reshape(flat), root_inverse)
    kid = lax.all_to_all(turned, "row", 0, 0, axis_index_groups=along)
    own = jnp.concatenate([kid.reshape(groups * half, rows), folded], axis=0)
    panel = lax.all_gather(own, "col", axis=0)
    keep = lax.dynamic_slice_in_dim(structure, lax.axis_index("row") * per, per, 1)
    mask = jnp.repeat(keep, BLK, axis=1).astype(dtype)
    masked = factor.transpose(1, 0, 2) * mask[:, :, None]
    row_m = lax.all_to_all(jnp.broadcast_to(masked[None], (n_row, kids, rows, cols)), "row", 0, 0)
    ainv, slots = pl.pallas_call(
        root_product,
        out_shape=(
            jax.ShapeDtypeStruct(flat, dtype),
            jax.ShapeDtypeStruct((groups, rows, cols), dtype),
        ),
        in_specs=[SMEM, ANY, ANY],
        out_specs=(VMEM, VMEM),
        scratch_shapes=[
            pltpu.VMEM((n_row, kids, rows, cols), dtype),
            pltpu.VMEM((n_col, rows // 2, 2 * cols), dtype),
            pltpu.VMEM((rows, kids * cols), jnp.float32),
            pltpu.VMEM(flat, jnp.float32),
            pltpu.SemaphoreType.DMA((2, CHUNKS)),
        ],
        compiler_params=pltpu.CompilerParams(vmem_limit_bytes=VMEM_ROOT << 20),
        cost_estimate=pl.CostEstimate(
            flops=2 * n_row * rows * rows * kids * cols,
            bytes_accessed=6 << 20,
            transcendentals=0,
        ),
    )(keep, row_m, panel)
    slots = lax.all_to_all(slots, "row", 0, 0, axis_index_groups=along)
    part = pl.pallas_call(
        kid_product,
        out_shape=jax.ShapeDtypeStruct((n_row, 2 * half, cols), dtype),
        in_specs=[VMEM, VMEM],
        out_specs=VMEM,
        compiler_params=pltpu.CompilerParams(vmem_limit_bytes=VMEM_KID << 20),
        cost_estimate=pl.CostEstimate(
            flops=2 * n_row * rows * rows * kids * cols,
            bytes_accessed=9 << 20,
            transcendentals=0,
        ),
    )(slots, panel)
    pieces = lax.all_to_all(part, "row", 0, 0)
    ainv_kk = pl.pallas_call(
        finish,
        out_shape=jax.ShapeDtypeStruct(flat, dtype),
        in_specs=[VMEM, VMEM],
        out_specs=VMEM,
        scratch_shapes=[pltpu.VMEM(flat, jnp.float32)],
        compiler_params=pltpu.CompilerParams(vmem_limit_bytes=6 << 20),
    )(pieces, inverse_diag.reshape(flat))
    return (ainv.reshape(factor.shape), ainv_kk.reshape(factor.shape))


def solution(mesh):
    return jax.shard_map(
        body,
        mesh=mesh,
        in_specs=(P("row", "col"), P("row", None, "col"), P("row", None, "col"), P()),
        out_specs=(P("row", None, "col"), P("row", None, "col")),
        check_vma=False,
    )
```

time: 157 us -> 154 us (0.981)
  blocking collectives: 98.6 us -> 95.8 us
  Pallas kernels: 13.7 us -> 11.6 us
  waiting for transfers between devices: 25.2 us -> 27 us
    all_to_all x2, blocking collectives: 22.8 us -> 30.3 us  [the longest x1 15.3 us: body(): kid = lax.all_to_all(turned, 'row', 0, 0, axis_index_groups=along)]
    all_to_all x1, blocking collectives: 20.5 us -> 14.6 us  [body(): pieces = lax.all_to_all(part, 'row', 0, 0)]
    all_to_all x1, blocking collectives: 55.3 us -> 50.8 us  [body(): lax.all_to_all(jnp.broadcast_to(masked[None], (n_row, kids, rows, cols)),...]
    pallas_call x2, Pallas kernels: 7.51 us -> 5.36 us  [the longest x1 3.51 us: body(): pl.pallas_call(kid_product, out_shape=jax.ShapeDtypeStruct((n_row, 2 * ha...]
    all_gather x1, waiting for transfers between devices: 25.1 us -> 27 us  [body(): panel = lax.all_gather(own, 'col', axis=0)]
where the time goes in v2:
time: 154 us; the launch traced here: 153 us
  blocking collectives  95.8 us (62%)
  waiting for transfers between devices  27 us (18%)
  between operations  14.1 us (9%)
  Pallas kernels  11.6 us (8%)
  other arithmetic  3.64 us (2%)
    all_to_all x1, blocking collectives, body(): lax.all_to_all(jnp.broadcast_to(masked[None], (n_row, kids, rows, cols)),...  50.8 us
    all_gather x1, waiting for transfers between devices, body(): panel = lax.all_gather(own, 'col', axis=0)  27 us
    all_to_all x1, blocking collectives, body(): kid = lax.all_to_all(turned, 'row', 0, 0, axis_index_groups=along)  15.3 us
    all_to_all x1, blocking collectives, body(): slots = lax.all_to_all(slots, 'row', 0, 0, axis_index_groups=along)  15 us
    all_to_all x1, blocking collectives, body(): pieces = lax.all_to_all(part, 'row', 0, 0)  14.6 us
    pallas_call x1, Pallas kernels, body(): pl.pallas_call(root_product, out_shape=(jax.ShapeDtypeStruct(flat, dtype)...  5.36 us
    pallas_call x1, Pallas kernels, body(): pl.pallas_call(kid_product, out_shape=jax.ShapeDtypeStruct((n_row, 2 * ha...  3.51 us
  transfers between devices with their start and end apart: 1, of which 1 were waited for; matrix products, arithmetic and copies ran while one was open for 2% of the time, Pallas kernels for 0%

profile of v2, /device:TPU:2, one launch (start us, length us, event | category | flops | bytes accessed | tf_op | source)
XLA Modules:
  0.0 153.3 jit_solution(9425125604648664648)
XLA Ops:
  7.2 0.0 all-gather.3.cloned.1.call-start
  7.2 1.8 %shard_map.59 = (bf16[8,64,256]{2,1,0:T(8,128)(2,1)}, bf16[128,256]{1,0:T(8,128)(2,1)}) custom-call(bf16[1024,128]{1,0:T(8,128)(2,1)} %bitcast.12, bf16[256,128]{1,0:T(8,128)(2,1)} %root_ref.1), custom_call_target="tpu_custom_call" | custom-call | tf_op jit(solution)/shard_map/pallas_call | solution.py:146
  9.1 15.3 %all_to_all.20 = bf16[8,64,256]{2,1,0:T(8,128)(2,1)S(1)} all-to-all(bf16[8,64,256]{2,1,0:T(8,128)(2,1)} %get-tuple-element.6), channel_id=1, replica_groups={{0,32,128,160,256,288,384,416},{64,96,192,224,320,352,448,480},{1,33,12..., dimensions={0} | all-to-all | bytes 524288 | tf_op jit(solution)/shard_map/all_to_all | solution.py:162
  24.4 1.6 %pad_maximum_fusion = bf16[640,256]{1,0:T(8,128)(2,1)} fusion(bf16[128,256]{1,0:T(8,128)(2,1)} %get-tuple-element.7, bf16[512,256]{1,0:T(8,128)(2,1)S(1)} %bitcast.13), kind=kLoop, calls=%fused_computation | loop fusion | flops 655360 | bytes 655360 | tf_op jit(solution)/shard_map/concatenate | solution.py:163
  26.0 0.0 all-gather.3.cloned.1.call-update
  26.0 0.8 fusion
  26.8 0.1 copy.8
  26.9 1.3 bitcast_multiply_fusion
  28.2 1.0 broadcast_in_dim.5
  29.3 50.8 %all_to_all.21.row_ref = bf16[16,4,256,128]{3,2,1,0:T(8,128)(2,1)} all-to-all(bf16[16,4,256,128]{3,2,1,0:T(8,128)(2,1)S(1)} %broadcast_in_dim.5), channel_id=1, replica_groups=mesh['row'=16,'col'=32] {'row'}, dimensions={0} | all-to-all | bytes 8388608 | tf_op jit(solution)/shard_map/all_to_all | solution.py:168
  80.1 27.0 %all-gather.3.cloned.1.call-done = bf16[20480,256]{1,0:T(8,128)(2,1)} async-done(((bf16[640,256]{1,0:T(8,128)(2,1)}), bf16[20480,256]{1,0:T(8,128)(2,1)}) %all-gather.3.cloned.1.call-update) | async-done | bytes 10485776 | tf_op jit(solution)/shard_map/all_gather | solution.py:164
  107.1 0.0 copy-start
  107.1 5.4 %shard_map.60 = (bf16[1024,128]{1,0:T(8,128)(2,1)}, bf16[8,256,128]{2,1,0:T(8,128)(2,1)S(1)}) custom-call(s32[4,2]{1,0:T(4,128)S(1)} %get-tuple-element.11.keep_ref, bf16[16,4,256,128]{3,2,1,0:T(8,128)(2,1)} %all_to_all.21.row_ref, bf16[32,640,256]{2,1,0:T(8,128)(2,1)} %bitcast.9), custom_call_target="tpu_custom_call" | custom-call | flops 1073741824 | bytes 6291456 | tf_op jit(solution)/shard_map/pallas_call | solution.py:169
  112.4 15.0 %all_to_all.22.slots_ref = bf16[8,256,128]{2,1,0:T(8,128)(2,1)S(1)} all-to-all(bf16[8,256,128]{2,1,0:T(8,128)(2,1)S(1)} %get-tuple-element.9), channel_id=1, replica_groups={{0,32,128,160,256,288,384,416},{64,96,192,224,320,352,448,480},{1,33,12..., dimensions={0} | all-to-all | bytes 1048576 | tf_op jit(solution)/shard_map/all_to_all | solution.py:191
  127.4 0.0 copy-done
  127.4 0.0 copy-start.1
  127.4 3.5 %shard_map.61 = bf16[16,128,128]{2,1,0:T(8,128)(2,1)S(1)} custom-call(bf16[8,256,128]{2,1,0:T(8,128)(2,1)S(1)} %all_to_all.22.slots_ref, bf16[32,640,256]{2,1,0:T(8,128)(2,1)S(1)} %bitcast.10), custom_call_target="tpu_custom_call" | custom-call | flops 1073741824 | bytes 9437184 | tf_op jit(solution)/shard_map/pallas_call | solution.py:192
  130.9 14.6 %all_to_all.23.pieces_ref = bf16[16,128,128]{2,1,0:T(8,128)(2,1)S(1)} all-to-all(bf16[16,128,128]{2,1,0:T(8,128)(2,1)S(1)} %shard_map.61), channel_id=1, replica_groups=mesh['row'=16,'col'=32] {'row'}, dimensions={0} | all-to-all | bytes 1048576 | tf_op jit(solution)/shard_map/all_to_all | solution.py:204
  145.6 0.0 copy-done.1
  145.6 0.9 shard_map.62
  (2 shorter events, 0.0 us)
Async XLA Ops:
  7.2 99.9 %all-gather.3.cloned.1.call-start = ((), (), s32[]{:S(2)}) async-start(), calls=%async_computation.4 | async-start | bytes 10813440 | tf_op jit(solution)/shard_map/all_gather | solution.py:164
  107.1 20.4 %copy-start = (bf16[20480,256]{1,0:T(8,128)(2,1)S(1)}, bf16[20480,256]{1,0:T(8,128)(2,1)}, u32[]{:S(2)}) copy-start(bf16[20480,256]{1,0:T(8,128)(2,1)} %all-gather.3.cloned.1.call-done) | copy-start | bytes 31457284
  127.4 18.1 %copy-start.1 = (bf16[256,4,128]{2,1,0:T(4,128)(2,1)S(1)}, bf16[256,4,128]{2,1,0:T(4,128)(2,1)}, u32[]{:S(2)}) copy-start(bf16[256,4,128]{2,1,0:T(4,128)(2,1)} %param.6) | copy-start | bytes 786436
Sparse Core Ops, SparseCore 0:
  26.1 80.9 all-gather.2

commit v3 on v2

--- a/solution.py
+++ b/solution.py
@@ -6,7 +6,8 @@
 from jax.sharding import PartitionSpec as P
 
 BLK = 128
-CHUNKS = 8
+CHUNKS = 4
+KID_CHUNKS = 2
 HALVES = 2
 VMEM_FIRST, VMEM_ROOT, VMEM_KID = 63, 50, 16
 ANY = pl.BlockSpec(memory_space=pl.ANY)
@@ -94,10 +95,10 @@
     groups, depth, cols = slots_ref.shape
     n_row, tall, _ = part_ref.shape
     half = cols // HALVES
-    c = panel_ref.shape[0] // CHUNKS
+    c = panel_ref.shape[0] // KID_CHUNKS
     right = slots_ref[...].reshape(groups * depth, cols)
 
-    @pl.loop(0, CHUNKS)
+    @pl.loop(0, KID_CHUNKS)
     def _(s):
         left = jnp.concatenate(
             [

time: 154 us -> 152 us (0.987)
  no operation moved by 1% of the time
where the time goes in v3:
time: 152 us
  blocking collectives  95.9 us (63%)
  waiting for transfers between devices  27 us (18%)
  between operations  14.1 us (9%)
  Pallas kernels  10.2 us (7%)
  other arithmetic  3.64 us (2%)
    all_to_all x1, blocking collectives, body(): lax.all_to_all(jnp.broadcast_to(masked[None], (n_row, kids, rows, cols)),...  50.8 us
    all_gather x1, waiting for transfers between devices, body(): panel = lax.all_gather(own, 'col', axis=0)  27 us
    all_to_all x1, blocking collectives, body(): kid = lax.all_to_all(turned, 'row', 0, 0, axis_index_groups=along)  15.3 us
    all_to_all x1, blocking collectives, body(): slots = lax.all_to_all(slots, 'row', 0, 0, axis_index_groups=along)  15 us
    all_to_all x1, blocking collectives, body(): pieces = lax.all_to_all(part, 'row', 0, 0)  14.7 us
    pallas_call x1, Pallas kernels, body(): pl.pallas_call(root_product, out_shape=(jax.ShapeDtypeStruct(flat, dtype)...  4.93 us
  transfers between devices with their start and end apart: 1, of which 1 were waited for; matrix products, arithmetic and copies ran while one was open for 2% of the time, Pallas kernels for 0%

profile of v3, /device:TPU:2, one launch (start us, length us, event | category | flops | bytes accessed | tf_op | source)
XLA Modules:
  0.0 152.0 jit_solution(5019986824825148763)
XLA Ops:
  7.2 0.0 all-gather.3.cloned.1.call-start
  7.2 1.8 %shard_map.59 = (bf16[8,64,256]{2,1,0:T(8,128)(2,1)}, bf16[128,256]{1,0:T(8,128)(2,1)}) custom-call(bf16[1024,128]{1,0:T(8,128)(2,1)} %bitcast.12, bf16[256,128]{1,0:T(8,128)(2,1)} %root_ref.1), custom_call_target="tpu_custom_call" | custom-call | tf_op jit(solution)/shard_map/pallas_call | solution.py:147
  9.1 15.3 %all_to_all.20 = bf16[8,64,256]{2,1,0:T(8,128)(2,1)S(1)} all-to-all(bf16[8,64,256]{2,1,0:T(8,128)(2,1)} %get-tuple-element.6), channel_id=1, replica_groups={{0,32,128,160,256,288,384,416},{64,96,192,224,320,352,448,480},{1,33,12..., dimensions={0} | all-to-all | bytes 524288 | tf_op jit(solution)/shard_map/all_to_all | solution.py:163
  24.4 1.6 %pad_maximum_fusion = bf16[640,256]{1,0:T(8,128)(2,1)} fusion(bf16[128,256]{1,0:T(8,128)(2,1)} %get-tuple-element.7, bf16[512,256]{1,0:T(8,128)(2,1)S(1)} %bitcast.13), kind=kLoop, calls=%fused_computation | loop fusion | flops 655360 | bytes 655360 | tf_op jit(solution)/shard_map/concatenate | solution.py:164
  26.0 0.0 all-gather.3.cloned.1.call-update
  26.0 0.8 fusion
  26.8 0.1 copy.8
  26.9 1.3 bitcast_multiply_fusion
  28.2 1.0 broadcast_in_dim.5
  29.3 50.8 %all_to_all.21.row_ref = bf16[16,4,256,128]{3,2,1,0:T(8,128)(2,1)} all-to-all(bf16[16,4,256,128]{3,2,1,0:T(8,128)(2,1)S(1)} %broadcast_in_dim.5), channel_id=1, replica_groups=mesh['row'=16,'col'=32] {'row'}, dimensions={0} | all-to-all | bytes 8388608 | tf_op jit(solution)/shard_map/all_to_all | solution.py:169
  80.1 27.0 %all-gather.3.cloned.1.call-done = bf16[20480,256]{1,0:T(8,128)(2,1)} async-done(((bf16[640,256]{1,0:T(8,128)(2,1)}), bf16[20480,256]{1,0:T(8,128)(2,1)}) %all-gather.3.cloned.1.call-update) | async-done | bytes 10485776 | tf_op jit(solution)/shard_map/all_gather | solution.py:165
  107.1 0.0 copy-start
  107.1 4.9 %shard_map.60 = (bf16[1024,128]{1,0:T(8,128)(2,1)}, bf16[8,256,128]{2,1,0:T(8,128)(2,1)S(1)}) custom-call(s32[4,2]{1,0:T(4,128)S(1)} %get-tuple-element.11.keep_ref, bf16[16,4,256,128]{3,2,1,0:T(8,128)(2,1)} %all_to_all.21.row_ref, bf16[32,640,256]{2,1,0:T(8,128)(2,1)} %bitcast.9), custom_call_target="tpu_custom_call" | custom-call | flops 1073741824 | bytes 6291456 | tf_op jit(solution)/shard_map/pallas_call | solution.py:170
  112.0 15.0 %all_to_all.22.slots_ref = bf16[8,256,128]{2,1,0:T(8,128)(2,1)S(1)} all-to-all(bf16[8,256,128]{2,1,0:T(8,128)(2,1)S(1)} %get-tuple-element.9), channel_id=1, replica_groups={{0,32,128,160,256,288,384,416},{64,96,192,224,320,352,448,480},{1,33,12..., dimensions={0} | all-to-all | bytes 1048576 | tf_op jit(solution)/shard_map/all_to_all | solution.py:192
  127.0 0.0 copy-done
  127.0 0.0 copy-start.1
  127.0 2.6 %shard_map.61 = bf16[16,128,128]{2,1,0:T(8,128)(2,1)S(1)} custom-call(bf16[8,256,128]{2,1,0:T(8,128)(2,1)S(1)} %all_to_all.22.slots_ref, bf16[32,640,256]{2,1,0:T(8,128)(2,1)S(1)} %bitcast.10), custom_call_target="tpu_custom_call" | custom-call | flops 1073741824 | bytes 9437184 | tf_op jit(solution)/shard_map/pallas_call | solution.py:193
  129.6 14.7 %all_to_all.23.pieces_ref = bf16[16,128,128]{2,1,0:T(8,128)(2,1)S(1)} all-to-all(bf16[16,128,128]{2,1,0:T(8,128)(2,1)S(1)} %shard_map.61), channel_id=1, replica_groups=mesh['row'=16,'col'=32] {'row'}, dimensions={0} | all-to-all | bytes 1048576 | tf_op jit(solution)/shard_map/all_to_all | solution.py:205
  144.3 0.0 copy-done.1
  144.3 0.9 shard_map.62
  (2 shorter events, 0.0 us)
Async XLA Ops:
  7.2 99.9 %all-gather.3.cloned.1.call-start = ((), (), s32[]{:S(2)}) async-start(), calls=%async_computation.4 | async-start | bytes 10813440 | tf_op jit(solution)/shard_map/all_gather | solution.py:165
  107.1 19.9 %copy-start = (bf16[20480,256]{1,0:T(8,128)(2,1)S(1)}, bf16[20480,256]{1,0:T(8,128)(2,1)}, u32[]{:S(2)}) copy-start(bf16[20480,256]{1,0:T(8,128)(2,1)} %all-gather.3.cloned.1.call-done) | copy-start | bytes 31457284
  127.0 17.3 %copy-start.1 = (bf16[256,4,128]{2,1,0:T(4,128)(2,1)S(1)}, bf16[256,4,128]{2,1,0:T(4,128)(2,1)}, u32[]{:S(2)}) copy-start(bf16[256,4,128]{2,1,0:T(4,128)(2,1)} %param.6) | copy-start | bytes 786436
Sparse Core Ops, SparseCore 0:
  26.1 80.9 all-gather.2

commit v4 on v3

--- a/solution.py
+++ b/solution.py
@@ -15,23 +15,32 @@
 SMEM = pl.BlockSpec(memory_space=pltpu.SMEM)
 
 
-def split_kids(flat_ref, root_ref, turned_ref, folded_ref, flat_buf, root_buf, wide_ref, sems):
-    groups, half, rows = turned_ref.shape
+def split_kids(
+    flat_ref, root_ref, turned_ref, own_ref, flat_buf, root_buf, folded_ref, wide_ref, turned_buf, sems
+):
+    groups, half, rows = turned_buf.shape
     kids = groups // HALVES
     cols = root_buf.shape[1]
     flat_copy = pltpu.make_async_copy(flat_ref, flat_buf, sems.at[0])
     root_copy = pltpu.make_async_copy(root_ref, root_buf, sems.at[1])
     flat_copy.start()
     root_copy.start()
+    root_copy.wait()
+    folded_ref[:, :cols] = root_buf[: rows // 2]
+    folded_ref[:, cols:] = root_buf[rows // 2 :]
+    at = pl.ds(own_ref.shape[0] - rows // 2, rows // 2)
+    own_copy = pltpu.make_async_copy(folded_ref, own_ref.at[at], sems.at[2])
+    own_copy.start()
     flat_copy.wait()
     wide_ref[...] = flat_buf[...].astype(jnp.float32)
     for n in range(kids):
         across = wide_ref[pl.ds(n, rows, stride=kids), :].astype(turned_ref.dtype).T
         for h in range(HALVES):
-            turned_ref[n * HALVES + h] = across[h * half : (h + 1) * half]
-    root_copy.wait()
-    folded_ref[:, :cols] = root_buf[: rows // 2]
-    folded_ref[:, cols:] = root_buf[rows // 2 :]
+            turned_buf[n * HALVES + h] = across[h * half : (h + 1) * half]
+    turned_copy = pltpu.make_async_copy(turned_buf, turned_ref, sems.at[3])
+    turned_copy.start()
+    own_copy.wait()
+    turned_copy.wait()
 
 
 def root_product(
@@ -144,24 +153,26 @@
         [y * side + x * HALVES + h for y in range(kids) for h in range(HALVES)]
         for x in range(side // HALVES)
     ]
-    turned, folded = pl.pallas_call(
+    turned, own = pl.pallas_call(
         split_kids,
         out_shape=(
             jax.ShapeDtypeStruct((groups, half, rows), dtype),
-            jax.ShapeDtypeStruct((rows // 2, 2 * cols), dtype),
+            jax.ShapeDtypeStruct((groups * half + rows // 2, rows), dtype),
         ),
         in_specs=[ANY, ANY],
-        out_specs=(VMEM, VMEM),
+        out_specs=(ANY, ANY),
         scratch_shapes=[
             pltpu.VMEM(flat, dtype),
             pltpu.VMEM((rows, cols), dtype),
+            pltpu.VMEM((rows // 2, 2 * cols), dtype),
             pltpu.VMEM(flat, jnp.float32),
-            pltpu.SemaphoreType.DMA((2,)),
+            pltpu.VMEM((groups, half, rows), dtype),
+            pltpu.SemaphoreType.DMA((4,)),
         ],
         compiler_params=pltpu.CompilerParams(vmem_limit_bytes=VMEM_FIRST << 20),
     )(factor.reshape(flat), root_inverse)
     kid = lax.all_to_all(turned, "row", 0, 0, axis_index_groups=along)
-    own = jnp.concatenate([kid.reshape(groups * half, rows), folded], axis=0)
+    own = lax.dynamic_update_slice(own, kid.reshape(groups * half, rows), (0, 0))
     panel = lax.all_gather(own, "col", axis=0)
     keep = lax.dynamic_slice_in_dim(structure, lax.axis_index("row") * per, per, 1)
     mask = jnp.repeat(keep, BLK, axis=1).astype(dtype)

time: 152 us -> 152 us (level)
  other arithmetic: 3.64 us -> 2.05 us
    concatenate x1 -> x0, other arithmetic: 1.59 us -> none  [body(): own = jnp.concatenate([kid.reshape(groups * half, rows), folded], axis=0)]
where the time goes in v4:
time: 152 us; the launch traced here: 151 us
  blocking collectives  95.9 us (63%)
  waiting for transfers between devices  27 us (18%)
  between operations  14.1 us (9%)
  Pallas kernels  10.2 us (7%)
  other arithmetic  2.05 us (1%)
  local copies, waits for them, and re-layouts  1.93 us (1%)
    all_to_all x1, blocking collectives, body(): lax.all_to_all(jnp.broadcast_to(masked[None], (n_row, kids, rows, cols)),...  50.8 us
    all_gather x1, waiting for transfers between devices, body(): panel = lax.all_gather(own, 'col', axis=0)  27 us
    all_to_all x1, blocking collectives, body(): kid = lax.all_to_all(turned, 'row', 0, 0, axis_index_groups=along)  15.3 us
    all_to_all x1, blocking collectives, body(): slots = lax.all_to_all(slots, 'row', 0, 0, axis_index_groups=along)  15.1 us
    all_to_all x1, blocking collectives, body(): pieces = lax.all_to_all(part, 'row', 0, 0)  14.6 us
    pallas_call x1, Pallas kernels, body(): pl.pallas_call(root_product, out_shape=(jax.ShapeDtypeStruct(flat, dtype)...  4.93 us
  transfers between devices with their start and end apart: 1, of which 1 were waited for; matrix products, arithmetic and copies ran while one was open for 2% of the time, Pallas kernels for 0%

profile of v4, /device:TPU:2, one launch (start us, length us, event | category | flops | bytes accessed | tf_op | source)
XLA Modules:
  0.0 151.2 jit_solution(14847659749362011045)
XLA Ops:
  7.2 0.0 all-gather.2.cloned.1.call-start
  7.2 1.8 %shard_map.59 = (bf16[8,64,256]{2,1,0:T(8,128)(2,1)}, bf16[640,256]{1,0:T(8,128)(2,1)}) custom-call(bf16[1024,128]{1,0:T(8,128)(2,1)} %bitcast.12, bf16[256,128]{1,0:T(8,128)(2,1)} %root_ref.1), custom_call_target="tpu_custom_call" | custom-call | tf_op jit(solution)/shard_map/pallas_call | solution.py:156
  9.1 15.3 %all_to_all.20 = bf16[8,64,256]{2,1,0:T(8,128)(2,1)S(1)} all-to-all(bf16[8,64,256]{2,1,0:T(8,128)(2,1)} %get-tuple-element.7), channel_id=1, replica_groups={{0,32,128,160,256,288,384,416},{64,96,192,224,320,352,448,480},{1,33,12..., dimensions={0} | all-to-all | bytes 524288 | tf_op jit(solution)/shard_map/all_to_all | solution.py:174
  24.4 0.7 bitcast_dynamic-update-slice_fusion
  25.1 0.0 all-gather.2.cloned.1.call-update
  25.2 0.8 fusion
  25.9 0.1 copy.10
  26.0 1.3 bitcast_multiply_fusion
  27.4 1.0 broadcast_in_dim.5
  28.4 50.8 %all_to_all.21.row_ref = bf16[16,4,256,128]{3,2,1,0:T(8,128)(2,1)} all-to-all(bf16[16,4,256,128]{3,2,1,0:T(8,128)(2,1)S(1)} %broadcast_in_dim.5), channel_id=1, replica_groups=mesh['row'=16,'col'=32] {'row'}, dimensions={0} | all-to-all | bytes 8388608 | tf_op jit(solution)/shard_map/all_to_all | solution.py:180
  79.2 27.0 %all-gather.2.cloned.1.call-done.panel_ref = bf16[32,640,256]{2,1,0:T(8,128)(2,1)} async-done(((bf16[1,640,256]{2,1,0:T(8,128)(2,1)}), bf16[32,640,256]{2,1,0:T(8,128)(2,1)}) %all-gather.2.cloned.1.call-update) | async-done | bytes 10485776 | tf_op jit(solution)/shard_map/all_gather | solution.py:176
  106.2 0.0 copy-start
  106.2 4.9 %shard_map.60 = (bf16[1024,128]{1,0:T(8,128)(2,1)}, bf16[8,256,128]{2,1,0:T(8,128)(2,1)S(1)}) custom-call(s32[4,2]{1,0:T(4,128)S(1)} %get-tuple-element.11.keep_ref, bf16[16,4,256,128]{3,2,1,0:T(8,128)(2,1)} %all_to_all.21.row_ref, bf16[32,640,256]{2,1,0:T(8,128)(2,1)} %all-gather.2.cloned.1.call-done.panel_ref), custom_call_target="tpu_custom_call" | custom-call | flops 1073741824 | bytes 6291456 | tf_op jit(solution)/shard_map/pallas_call | solution.py:181
  111.2 15.1 %all_to_all.22.slots_ref = bf16[8,256,128]{2,1,0:T(8,128)(2,1)S(1)} all-to-all(bf16[8,256,128]{2,1,0:T(8,128)(2,1)S(1)} %get-tuple-element.9), channel_id=1, replica_groups={{0,32,128,160,256,288,384,416},{64,96,192,224,320,352,448,480},{1,33,12..., dimensions={0} | all-to-all | bytes 1048576 | tf_op jit(solution)/shard_map/all_to_all | solution.py:203
  126.3 0.0 copy-done
  126.3 0.0 copy-start.1
  126.3 2.6 %shard_map.61 = bf16[16,128,128]{2,1,0:T(8,128)(2,1)S(1)} custom-call(bf16[8,256,128]{2,1,0:T(8,128)(2,1)S(1)} %all_to_all.22.slots_ref, bf16[32,640,256]{2,1,0:T(8,128)(2,1)S(1)} %copy-done), custom_call_target="tpu_custom_call" | custom-call | flops 1073741824 | bytes 9437184 | tf_op jit(solution)/shard_map/pallas_call | solution.py:204
  128.8 14.6 %all_to_all.23.pieces_ref = bf16[16,128,128]{2,1,0:T(8,128)(2,1)S(1)} all-to-all(bf16[16,128,128]{2,1,0:T(8,128)(2,1)S(1)} %shard_map.61), channel_id=1, replica_groups=mesh['row'=16,'col'=32] {'row'}, dimensions={0} | all-to-all | bytes 1048576 | tf_op jit(solution)/shard_map/all_to_all | solution.py:216
  143.5 0.0 copy-done.1
  143.5 0.9 shard_map.62
  (2 shorter events, 0.0 us)
Async XLA Ops:
  7.2 99.1 %all-gather.2.cloned.1.call-start = ((), (), s32[]{:S(2)}) async-start(), calls=%async_computation.4 | async-start | bytes 10813440 | tf_op jit(solution)/shard_map/all_gather | solution.py:176
  106.2 20.1 %copy-start = (bf16[32,640,256]{2,1,0:T(8,128)(2,1)S(1)}, bf16[32,640,256]{2,1,0:T(8,128)(2,1)}, u32[]{:S(2)}) copy-start(bf16[32,640,256]{2,1,0:T(8,128)(2,1)} %all-gather.2.cloned.1.call-done.panel_ref) | copy-start | bytes 31457284
  126.3 17.2 %copy-start.1 = (bf16[256,4,128]{2,1,0:T(4,128)(2,1)S(1)}, bf16[256,4,128]{2,1,0:T(4,128)(2,1)}, u32[]{:S(2)}) copy-start(bf16[256,4,128]{2,1,0:T(4,128)(2,1)} %param.6) | copy-start | bytes 786436
Sparse Core Ops, SparseCore 0:
  25.3 80.9 all-gather.1

commit v5 on v4

--- a/solution.py
+++ b/solution.py
@@ -44,7 +44,7 @@
 
 
 def root_product(
-    keep_ref, row_ref, panel_ref, ainv_ref, slots_ref, row_buf, root_buf, acc_ref, wide_ref, sems
+    keep_ref, row_ref, panel_ref, ainv_ref, slots_ref, row_buf, root_buf, acc_ref, wide_ref, ainv_buf, sems, out_sem
 ):
     n_row, kids, depth, cols = row_buf.shape
     first = panel_ref.shape[1] - root_buf.shape[1]
@@ -92,12 +92,17 @@
     for n in range(kids):
         value = (-acc_ref[:, n * cols : (n + 1) * cols]).astype(slots_ref.dtype)
         wide_ref[pl.ds(n, depth, stride=kids), :] = value.astype(jnp.float32)
+    ainv_buf[...] = wide_ref[...].astype(ainv_buf.dtype)
+    ainv_copy = pltpu.make_async_copy(ainv_buf, ainv_ref, out_sem)
+    ainv_copy.start()
+    for n in range(kids):
+        value = (-acc_ref[:, n * cols : (n + 1) * cols]).astype(slots_ref.dtype)
         for b in range(depth // BLK):
             at = slice(b * BLK, (b + 1) * BLK)
             kept = jnp.where(keep_ref[n, b] != 0, value[at], 0).astype(slots_ref.dtype)
             for h in range(HALVES):
                 slots_ref[n * HALVES + h, at] = kept
-    ainv_ref[...] = wide_ref[...].astype(ainv_ref.dtype)
+    ainv_copy.wait()
 
 
 def kid_product(slots_ref, panel_ref, part_ref):
@@ -185,13 +190,15 @@
             jax.ShapeDtypeStruct((groups, rows, cols), dtype),
         ),
         in_specs=[SMEM, ANY, ANY],
-        out_specs=(VMEM, VMEM),
+        out_specs=(ANY, VMEM),
         scratch_shapes=[
             pltpu.VMEM((n_row, kids, rows, cols), dtype),
             pltpu.VMEM((n_col, rows // 2, 2 * cols), dtype),
             pltpu.VMEM((rows, kids * cols), jnp.float32),
             pltpu.VMEM(flat, jnp.float32),
+            pltpu.VMEM(flat, dtype),
             pltpu.SemaphoreType.DMA((2, CHUNKS)),
+            pltpu.SemaphoreType.DMA(()),
         ],
         compiler_params=pltpu.CompilerParams(vmem_limit_bytes=VMEM_ROOT << 20),
         cost_estimate=pl.CostEstimate(

time: 152 us -> 152 us (level)
  no operation moved by 1% of the time
where the time goes in v5:
time: 152 us; the launch traced here: 151 us
  blocking collectives  95.9 us (63%)
  waiting for transfers between devices  27 us (18%)
  between operations  14.1 us (9%)
  Pallas kernels  10.2 us (7%)
  other arithmetic  2.05 us (1%)
  local copies, waits for them, and re-layouts  1.93 us (1%)
    all_to_all x1, blocking collectives, body(): lax.all_to_all(jnp.broadcast_to(masked[None], (n_row, kids, rows, cols)),...  50.8 us
    all_gather x1, waiting for transfers between devices, body(): panel = lax.all_gather(own, 'col', axis=0)  27 us
    all_to_all x1, blocking collectives, body(): kid = lax.all_to_all(turned, 'row', 0, 0, axis_index_groups=along)  15.3 us
    all_to_all x1, blocking collectives, body(): slots = lax.all_to_all(slots, 'row', 0, 0, axis_index_groups=along)  15.1 us
    all_to_all x1, blocking collectives, body(): pieces = lax.all_to_all(part, 'row', 0, 0)  14.6 us
    pallas_call x1, Pallas kernels, body(): pl.pallas_call(root_product, out_shape=(jax.ShapeDtypeStruct(flat, dtype)...  4.91 us
  transfers between devices with their start and end apart: 1, of which 1 were waited for; matrix products, arithmetic and copies ran while one was open for 2% of the time, Pallas kernels for 0%

profile of v5, /device:TPU:2, one launch (start us, length us, event | category | flops | bytes accessed | tf_op | source)
XLA Modules:
  0.0 151.1 jit_solution(4296134294566699106)
XLA Ops:
  7.2 0.0 all-gather.2.cloned.1.call-start
  7.2 1.8 %shard_map.59 = (bf16[8,64,256]{2,1,0:T(8,128)(2,1)}, bf16[640,256]{1,0:T(8,128)(2,1)}) custom-call(bf16[1024,128]{1,0:T(8,128)(2,1)} %bitcast.12, bf16[256,128]{1,0:T(8,128)(2,1)} %root_ref.1), custom_call_target="tpu_custom_call" | custom-call | tf_op jit(solution)/shard_map/pallas_call | solution.py:161
  9.1 15.3 %all_to_all.20 = bf16[8,64,256]{2,1,0:T(8,128)(2,1)S(1)} all-to-all(bf16[8,64,256]{2,1,0:T(8,128)(2,1)} %get-tuple-element.7), channel_id=1, replica_groups={{0,32,128,160,256,288,384,416},{64,96,192,224,320,352,448,480},{1,33,12..., dimensions={0} | all-to-all | bytes 524288 | tf_op jit(solution)/shard_map/all_to_all | solution.py:179
  24.4 0.7 bitcast_dynamic-update-slice_fusion
  25.1 0.0 all-gather.2.cloned.1.call-update
  25.2 0.8 fusion
  25.9 0.1 copy.10
  26.0 1.3 bitcast_multiply_fusion
  27.4 1.0 broadcast_in_dim.5
  28.4 50.8 %all_to_all.21.row_ref = bf16[16,4,256,128]{3,2,1,0:T(8,128)(2,1)} all-to-all(bf16[16,4,256,128]{3,2,1,0:T(8,128)(2,1)S(1)} %broadcast_in_dim.5), channel_id=1, replica_groups=mesh['row'=16,'col'=32] {'row'}, dimensions={0} | all-to-all | bytes 8388608 | tf_op jit(solution)/shard_map/all_to_all | solution.py:185
  79.2 27.0 %all-gather.2.cloned.1.call-done.panel_ref = bf16[32,640,256]{2,1,0:T(8,128)(2,1)} async-done(((bf16[1,640,256]{2,1,0:T(8,128)(2,1)}), bf16[32,640,256]{2,1,0:T(8,128)(2,1)}) %all-gather.2.cloned.1.call-update) | async-done | bytes 10485776 | tf_op jit(solution)/shard_map/all_gather | solution.py:181
  106.2 0.0 copy-start
  106.2 4.9 %shard_map.60 = (bf16[1024,128]{1,0:T(8,128)(2,1)}, bf16[8,256,128]{2,1,0:T(8,128)(2,1)S(1)}) custom-call(s32[4,2]{1,0:T(4,128)S(1)} %get-tuple-element.11.keep_ref, bf16[16,4,256,128]{3,2,1,0:T(8,128)(2,1)} %all_to_all.21.row_ref, bf16[32,640,256]{2,1,0:T(8,128)(2,1)} %all-gather.2.cloned.1.call-done.panel_ref), custom_call_target="tpu_custom_call" | custom-call | flops 1073741824 | bytes 6291456 | tf_op jit(solution)/shard_map/pallas_call | solution.py:186
  111.1 15.1 %all_to_all.22.slots_ref = bf16[8,256,128]{2,1,0:T(8,128)(2,1)S(1)} all-to-all(bf16[8,256,128]{2,1,0:T(8,128)(2,1)S(1)} %get-tuple-element.9), channel_id=1, replica_groups={{0,32,128,160,256,288,384,416},{64,96,192,224,320,352,448,480},{1,33,12..., dimensions={0} | all-to-all | bytes 1048576 | tf_op jit(solution)/shard_map/all_to_all | solution.py:210
  126.3 0.0 copy-done
  126.3 0.0 copy-start.1
  126.3 2.6 %shard_map.61 = bf16[16,128,128]{2,1,0:T(8,128)(2,1)S(1)} custom-call(bf16[8,256,128]{2,1,0:T(8,128)(2,1)S(1)} %all_to_all.22.slots_ref, bf16[32,640,256]{2,1,0:T(8,128)(2,1)S(1)} %copy-done), custom_call_target="tpu_custom_call" | custom-call | flops 1073741824 | bytes 9437184 | tf_op jit(solution)/shard_map/pallas_call | solution.py:211
  128.8 14.6 %all_to_all.23.pieces_ref = bf16[16,128,128]{2,1,0:T(8,128)(2,1)S(1)} all-to-all(bf16[16,128,128]{2,1,0:T(8,128)(2,1)S(1)} %shard_map.61), channel_id=1, replica_groups=mesh['row'=16,'col'=32] {'row'}, dimensions={0} | all-to-all | bytes 1048576 | tf_op jit(solution)/shard_map/all_to_all | solution.py:223
  143.4 0.0 copy-done.1
  143.4 0.9 shard_map.62
  (2 shorter events, 0.0 us)
Async XLA Ops:
  7.2 99.1 %all-gather.2.cloned.1.call-start = ((), (), s32[]{:S(2)}) async-start(), calls=%async_computation.4 | async-start | bytes 10813440 | tf_op jit(solution)/shard_map/all_gather | solution.py:181
  106.2 20.0 %copy-start = (bf16[32,640,256]{2,1,0:T(8,128)(2,1)S(1)}, bf16[32,640,256]{2,1,0:T(8,128)(2,1)}, u32[]{:S(2)}) copy-start(bf16[32,640,256]{2,1,0:T(8,128)(2,1)} %all-gather.2.cloned.1.call-done.panel_ref) | copy-start | bytes 31457284
  126.3 17.2 %copy-start.1 = (bf16[256,4,128]{2,1,0:T(4,128)(2,1)S(1)}, bf16[256,4,128]{2,1,0:T(4,128)(2,1)}, u32[]{:S(2)}) copy-start(bf16[256,4,128]{2,1,0:T(4,128)(2,1)} %param.6) | copy-start | bytes 786436
Sparse Core Ops, SparseCore 0:
  25.3 80.9 all-gather.1
